TPU v7x, 1024 devices: a whole 4x8x16 slice. The times are simulated.
1024 devices in a mesh: sa: 32 (over y, x), gx: 8 (over z_lo, core), gy: 4 (over z_hi).
Axes of the slice: x: 4, y: 8, z: 16 (z_hi: 4, z_lo: 4; z = z_hi * 4 + z_lo), core: 2. Of those that a mesh axis runs over, the one named last changes fastest.
Arguments:
- vectors: float32 [32, 16, 8, 24, 256], P('sa', 'gx', 'gy'), may hold values from -6 to 6
- gauge_links: float32 [16, 8, 72, 256], P('gx', 'gy'), may hold values from -1 to 1, as said below
Outputs:
- filtered_once: float32 [32, 16, 8, 24, 256], P('sa', 'gx', 'gy')
- filtered_twice: float32 [32, 16, 8, 24, 256], P('sa', 'gx', 'gy')
Inputs may be any that keep to these rules, and one draw needn't show every extreme that they name: `gauge_links`: for each site and direction the nine complex entries form a special unitary 3 x 3 matrix.
All inputs are finite; a program needn't handle non-finite values.
Results may differ from a plain program's by a relative error of at most 0.0001.
Values sent between devices are 32-bit elements; how exact they have to be, the bound alone decides.
A program may use at most 32 MiB of HBM per device.

v0:
```python
import jax
import jax.numpy as jnp
from jax import lax
from jax.sharding import PartitionSpec as P

NT = 64


m5_height = 1.8
wall_mass = 0.1
cheb_scale = 0.2
cheb_shift = -0.5
gamma_source = ((3, 2, 1, 0), (3, 2, 1, 0), (2, 3, 0, 1), (2, 3, 0, 1))
gamma_real = ((0, 0, 0, 0), (-1, 1, 1, -1), (0, 0, 0, 0), (1, 1, 1, 1))
gamma_imag = ((-1, -1, 1, 1), (0, 0, 0, 0), (-1, 1, 1, -1), (0, 0, 0, 0))


def padded(shard, sides, width):
    for axis, dim in sides:
        devices, length = (lax.axis_size(axis), shard.shape[dim])
        up = [(i, (i + 1) % devices) for i in range(devices)]
        down = [(j, i) for i, j in up]
        last = lax.slice_in_dim(shard, length - width, length, axis=dim)
        first = lax.slice_in_dim(shard, 0, width, axis=dim)
        before = lax.ppermute(last, axis, up)
        after = lax.ppermute(first, axis, down)
        shard = jnp.concatenate([before, shard, after], axis=dim)
    return shard


def shifted(value, axis, steps):
    count = lax.axis_size(axis)
    pairs = [(source, (source + steps) % count) for source in range(count)]
    return lax.ppermute(value, axis, pairs)


def split_spin(spinor):
    return spinor.reshape(spinor.shape[:-2] + (4, 2, 3, spinor.shape[-1]))


def join_spin(spinor):
    return spinor.reshape(spinor.shape[:-4] + (24, spinor.shape[-1]))


def gamma_times(spinor, direction, sign):
    pieces = []
    for spin_index in range(4):
        source = spinor[..., gamma_source[direction][spin_index], :, :, :]
        own_spin = spinor[..., spin_index, :, :, :]
        coef_re = sign * gamma_real[direction][spin_index]
        coef_im = sign * gamma_imag[direction][spin_index]
        new_re = (
            own_spin[..., 0, :, :] + coef_re * source[..., 0, :, :] - coef_im * source[..., 1, :, :]
        )
        new_im = (
            own_spin[..., 1, :, :] + coef_re * source[..., 1, :, :] + coef_im * source[..., 0, :, :]
        )
        pieces.append(jnp.stack([new_re, new_im], axis=-3))
    return jnp.stack(pieces, axis=-4)


def colour_times(link_dir, spinor, adjoint):
    link_re = link_dir[:, :, 0]
    link_im = link_dir[:, :, 1]
    if adjoint:
        link_re = jnp.swapaxes(link_re, 2, 3)
        link_im = -jnp.swapaxes(link_im, 2, 3)
    link_re = link_re[None, :, :, None]
    link_im = link_im[None, :, :, None]
    spin_re = spinor[..., 0, :, :][..., None, :, :]
    spin_im = spinor[..., 1, :, :][..., None, :, :]
    out_re = jnp.sum(link_re * spin_re - link_im * spin_im, axis=-2)
    out_im = jnp.sum(link_re * spin_im + link_im * spin_re, axis=-2)
    return jnp.stack([out_re, out_im], axis=-3)


def along_local(spinor, direction, stride):
    local_cells = spinor.shape[-1]
    if direction == 2:
        return jnp.roll(spinor, -stride * NT, axis=-1)
    time_index = jnp.arange(local_cells, dtype=jnp.int32) % NT
    if stride == 1:
        return jnp.where(
            time_index == NT - 1, -jnp.roll(spinor, NT - 1, axis=-1), jnp.roll(spinor, -1, axis=-1)
        )
    return jnp.where(
        time_index == 0, -jnp.roll(spinor, 1 - NT, axis=-1), jnp.roll(spinor, 1, axis=-1)
    )


def hopping_local(spinor_rows, gauge):
    spinor = split_spin(spinor_rows)
    hop_sum = jnp.zeros_like(spinor)
    for direction in range(4):
        link_dir = gauge[:, :, direction]
        packed = gamma_times(spinor, direction, -1) + colour_times(
            link_dir, gamma_times(spinor, direction, 1), True
        )
        if direction == 0:
            rimmed = padded(join_spin(packed), (("gx", 1),), 1)
            ahead_site = split_spin(rimmed[:, 2:])
            behind_site = split_spin(rimmed[:, :-2])
        elif direction == 1:
            rimmed = padded(join_spin(packed), (("gy", 2),), 1)
            ahead_site = split_spin(rimmed[:, :, 2:])
            behind_site = split_spin(rimmed[:, :, :-2])
        else:
            ahead_site = along_local(packed, direction, 1)
            behind_site = along_local(packed, direction, -1)
        forward = colour_times(link_dir, gamma_times(ahead_site, direction, -1), False)
        hop_sum = hop_sum + 0.5 * forward + 0.5 * gamma_times(behind_site, direction, 1)
    return join_spin(-0.5 * hop_sum)


def chiral_local(members, flips):
    position = lax.axis_index("sa")
    last_index = lax.axis_size("sa") - 1
    received = []
    for offset in (1, -1):
        pieces = []
        for spinor, flipped in zip(members, flips):
            edge_slice = spinor if offset == 1 else spinor
            if (offset == 1) != flipped:
                pieces.append(edge_slice[:, :, :, :12])
            else:
                pieces.append(edge_slice[:, :, :, 12:])
        received.append(shifted(pieces[0], "sa", offset))
    prior_scale = jnp.where(position == 0, -wall_mass, 1.0)
    next_scale = jnp.where(position == last_index, -wall_mass, 1.0)
    results = []
    for member_index, (spinor, flipped) in enumerate(zip(members, flips)):
        prior_edge = prior_scale * received[0]
        next_edge = next_scale * received[1]
        upper_half = jnp.concatenate([spinor[1:, :, :, :12], next_edge], axis=0)
        lower_half = jnp.concatenate([prior_edge, spinor[:-1, :, :, 12:]], axis=0)
        results.append(jnp.concatenate([upper_half, lower_half], axis=3))
    return results


def gamma_five(spinor):
    return jnp.concatenate([spinor[:, :, :, :12], -spinor[:, :, :, 12:]], axis=3)


def mirror(spinor):
    flat = spinor.reshape(
        spinor.shape[0], spinor.shape[1] * spinor.shape[2] * spinor.shape[3], spinor.shape[4]
    )
    slab_rows = lax.all_to_all(flat, "sa", split_axis=1, concat_axis=0, tiled=True)
    slab_rows = slab_rows[::-1]
    restored = lax.all_to_all(slab_rows, "sa", split_axis=0, concat_axis=1, tiled=True)
    return restored.reshape(spinor.shape)


def flipped_dirac(mirrored, gauge):
    return (
        (5.0 - m5_height) * mirrored
        + hopping_local(mirrored, gauge)
        - chiral_local((mirrored,), (True,))[0]
    )


def hermitian_local(spinor, gauge):
    return gamma_five(flipped_dirac(mirror(spinor), gauge))


def per_device(vectors, gauge_links):
    gauge = gauge_links.reshape(gauge_links.shape[:2] + (4, 2, 3, 3, gauge_links.shape[-1]))
    filtered_once = cheb_scale * hermitian_local(vectors, gauge) + cheb_shift * vectors
    filtered_twice = (
        2.0 * (cheb_scale * hermitian_local(filtered_once, gauge) + cheb_shift * filtered_once)
        - vectors
    )
    return (filtered_once, filtered_twice)


def solution(mesh):
    placed = (P("sa", "gx", "gy", None, None), P("gx", "gy", None, None))
    return jax.shard_map(
        per_device,
        mesh=mesh,
        in_specs=placed,
        out_specs=(P("sa", "gx", "gy", None, None), P("sa", "gx", "gy", None, None)),
        check_vma=False,
    )
```

profile of v0, /device:TPU:1, one launch (start us, length us, event | category | flops | bytes accessed | tf_op | source)
XLA Modules:
  0.0 147.2 jit_solution(600013259601671442)
XLA Ops:
  0.6 1.7 %reshape.4009 = f32[1,96,256]{2,0,1:T(1,128)} reshape(f32[1,2,2,24,256]{4,3,2,1,0:T(8,128)} %param.2) | data formatting | bytes 196608 | tf_op jit(solution)/shard_map/reshape | solution.py:145
  2.3 10.5 %all-to-all-start = ((f32[1,96,256]{2,0,1:T(1,128)}), f32[1,96,256]{2,0,1:T(1,128)S(1)}, u32[]{:S(2)}, u32[]{:S(2)}) async-start(f32[1,96,256]{2,0,1:T(1,128)} %reshape.4009), calls=%async_computation | async-start | bytes 196608 | tf_op jit(solution)/shard_map/all_to_all | solution.py:148
  13.6 8.3 %all-to-all-done = f32[1,96,256]{2,0,1:T(1,128)S(1)} async-done(((f32[1,96,256]{2,0,1:T(1,128)}), f32[1,96,256]{2,0,1:T(1,128)S(1)}, u32[]{:S(2)}, u32[]{:S(2)}) %all-to-all-start) | async-done | bytes 98336 | tf_op jit(solution)/shard_map/all_to_all | solution.py:148
  22.2 0.7 rev.6
  22.9 3.8 %all-to-all-start.1 = ((f32[32,3,256]{2,1,0:T(4,128)}), f32[32,3,256]{2,1,0:T(4,128)S(1)}, u32[]{:S(2)}, u32[]{:S(2)}) async-start(f32[32,3,256]{2,1,0:T(4,128)} %rev.6), calls=%async_computation.1 | async-start | bytes 262144 | tf_op jit(solution)/shard_map/all_to_all | solution.py:150
  26.7 9.4 %all-to-all-done.1 = f32[32,3,256]{2,1,0:T(4,128)S(1)} async-done(((f32[32,3,256]{2,1,0:T(4,128)}), f32[32,3,256]{2,1,0:T(4,128)S(1)}, u32[]{:S(2)}, u32[]{:S(2)}) %all-to-all-start.1) | async-done | bytes 98336 | tf_op jit(solution)/shard_map/all_to_all | solution.py:150
  40.8 17.9 %collective-permute-start.2 = (f32[1,2,1,24,256]{4,2,3,1,0:T(1,128)S(1)}, f32[1,2,1,24,256]{4,2,3,1,0:T(1,128)S(1)}, u32[]{:S(2)}, u32[]{:S(2)}) collective-permute-start(f32[1,2,1,24,256]{4,2,3,1,0:T(1,128)S(1)} %get-tuple-element.171), channel_id=1, source_target_pairs={{1,0},{2,1},{3,2},{0,3},{5,4},{6,5},{7,6},{4,7},{9,8},{10,9},{11,1... | collective-permute-start | bytes 147464 | tf_op jit(solution)/shard_map/ppermute | solution.py:26
  58.8 1.9 %collective-permute-start.3 = (f32[1,2,1,24,256]{4,2,3,1,0:T(1,128)S(1)}, f32[1,2,1,24,256]{4,2,3,1,0:T(1,128)S(1)}, u32[]{:S(2)}, u32[]{:S(2)}) collective-permute-start(f32[1,2,1,24,256]{4,2,3,1,0:T(1,128)S(1)} %get-tuple-element.170), channel_id=1, source_target_pairs={{0,1},{1,2},{2,3},{3,0},{4,5},{5,6},{6,7},{7,4},{8,9},{9,10},{10,1... | collective-permute-start | bytes 147464 | tf_op jit(solution)/shard_map/ppermute | solution.py:25
  61.6 5.5 %collective-permute-start = (f32[1,1,2,24,256]{4,2,3,1,0:T(2,128)S(1)}, f32[1,1,2,24,256]{4,2,3,1,0:T(2,128)S(1)}, u32[]{:S(2)}, u32[]{:S(2)}) collective-permute-start(f32[1,1,2,24,256]{4,2,3,1,0:T(2,128)S(1)} %get-tuple-element.183), channel_id=1, source_target_pairs={{4,0},{8,4},{12,8},{16,12},{20,16},{24,20},{28,24},{0,28},{5,1},{9... | collective-permute-start | bytes 147464 | tf_op jit(solution)/shard_map/ppermute | solution.py:26
  67.0 3.0 %collective-permute-start.1 = (f32[1,1,2,24,256]{4,2,3,1,0:T(2,128)S(1)}, f32[1,1,2,24,256]{4,2,3,1,0:T(2,128)S(1)}, u32[]{:S(2)}, u32[]{:S(2)}) collective-permute-start(f32[1,1,2,24,256]{4,2,3,1,0:T(2,128)S(1)} %get-tuple-element.182), channel_id=1, source_target_pairs={{0,4},{4,8},{8,12},{12,16},{16,20},{20,24},{24,28},{28,0},{1,5},{5... | collective-permute-start | bytes 147464 | tf_op jit(solution)/shard_map/ppermute | solution.py:25
  70.1 1.9 %collective-permute-start.5 = (f32[1,2,2,12,256]{4,3,2,1,0:T(8,128)S(1)}, f32[1,2,2,12,256]{4,3,2,1,0:T(8,128)S(1)}, u32[]{:S(2)}, u32[]{:S(2)}) collective-permute-start(f32[1,2,2,12,256]{4,3,2,1,0:T(8,128)S(1)} %get-tuple-element.189), channel_id=1, source_target_pairs={{0,32},{32,64},{64,96},{96,128},{128,160},{160,192},{192,224},{224... | collective-permute-start | bytes 147464 | tf_op jit(solution)/shard_map/ppermute | solution.py:34
  72.3 6.7 %collective-permute-start.4 = (f32[1,2,2,12,256]{4,3,2,1,0:T(8,128)S(1)}, f32[1,2,2,12,256]{4,3,2,1,0:T(8,128)S(1)}, u32[]{:S(2)}, u32[]{:S(2)}) collective-permute-start(f32[1,2,2,12,256]{4,3,2,1,0:T(8,128)S(1)} %get-tuple-element.188), channel_id=1, source_target_pairs={{0,992},{32,0},{64,32},{96,64},{128,96},{160,128},{192,160},{224,1... | collective-permute-start | bytes 147464 | tf_op jit(solution)/shard_map/ppermute | solution.py:34
  81.0 0.4 fusion.10
  81.6 0.9 copy-done
  82.6 15.2 %all_to_all.42 = f32[1,96,256]{2,0,1:T(1,128)S(1)} all-to-all(f32[1,96,256]{2,0,1:T(1,128)S(1)} %copy.4488), channel_id=1, replica_groups=mesh['sa'=32,'gx'=8,'gy'=4] {'sa'}, dimensions={1} | all-to-all | bytes 196608 | tf_op jit(solution)/shard_map/all_to_all | solution.py:148
  98.2 12.6 %all_to_all.43 = f32[32,3,256]{2,1,0:T(4,128)S(1)} all-to-all(f32[32,3,256]{2,1,0:T(4,128)S(1)} %rev.7), channel_id=1, replica_groups=mesh['sa'=32,'gx'=8,'gy'=4] {'sa'}, dimensions={0} | all-to-all | bytes 196608 | tf_op jit(solution)/shard_map/all_to_all | solution.py:150
  115.4 7.5 %collective-permute-start.8 = (f32[1,2,1,24,256]{4,2,3,1,0:T(1,128)S(1)}, f32[1,2,1,24,256]{4,2,3,1,0:T(1,128)S(1)}, u32[]{:S(2)}, u32[]{:S(2)}) collective-permute-start(f32[1,2,1,24,256]{4,2,3,1,0:T(1,128)S(1)} %get-tuple-element.143), channel_id=1, source_target_pairs={{1,0},{2,1},{3,2},{0,3},{5,4},{6,5},{7,6},{4,7},{9,8},{10,9},{11,1... | collective-permute-start | bytes 147464 | tf_op jit(solution)/shard_map/ppermute | solution.py:26
  123.0 1.9 %collective-permute-start.9 = (f32[1,2,1,24,256]{4,2,3,1,0:T(1,128)S(1)}, f32[1,2,1,24,256]{4,2,3,1,0:T(1,128)S(1)}, u32[]{:S(2)}, u32[]{:S(2)}) collective-permute-start(f32[1,2,1,24,256]{4,2,3,1,0:T(1,128)S(1)} %get-tuple-element.142), channel_id=1, source_target_pairs={{0,1},{1,2},{2,3},{3,0},{4,5},{5,6},{6,7},{7,4},{8,9},{9,10},{10,1... | collective-permute-start | bytes 147464 | tf_op jit(solution)/shard_map/ppermute | solution.py:25
  125.5 5.4 %collective-permute-start.6 = (f32[1,1,2,24,256]{4,2,3,1,0:T(2,128)S(1)}, f32[1,1,2,24,256]{4,2,3,1,0:T(2,128)S(1)}, u32[]{:S(2)}, u32[]{:S(2)}) collective-permute-start(f32[1,1,2,24,256]{4,2,3,1,0:T(2,128)S(1)} %get-tuple-element.155), channel_id=1, source_target_pairs={{4,0},{8,4},{12,8},{16,12},{20,16},{24,20},{28,24},{0,28},{5,1},{9... | collective-permute-start | bytes 147464 | tf_op jit(solution)/shard_map/ppermute | solution.py:26
  131.0 3.0 %collective-permute-start.7 = (f32[1,1,2,24,256]{4,2,3,1,0:T(2,128)S(1)}, f32[1,1,2,24,256]{4,2,3,1,0:T(2,128)S(1)}, u32[]{:S(2)}, u32[]{:S(2)}) collective-permute-start(f32[1,1,2,24,256]{4,2,3,1,0:T(2,128)S(1)} %get-tuple-element.154), channel_id=1, source_target_pairs={{0,4},{4,8},{8,12},{12,16},{16,20},{20,24},{24,28},{28,0},{1,5},{5... | collective-permute-start | bytes 147464 | tf_op jit(solution)/shard_map/ppermute | solution.py:25
  134.3 3.0 %collective-permute-start.10 = (f32[1,2,2,12,256]{4,3,2,1,0:T(8,128)S(1)}, f32[1,2,2,12,256]{4,3,2,1,0:T(8,128)S(1)}, u32[]{:S(2)}, u32[]{:S(2)}) collective-permute-start(f32[1,2,2,12,256]{4,3,2,1,0:T(8,128)S(1)} %get-tuple-element.160), channel_id=1, source_target_pairs={{0,992},{32,0},{64,32},{96,64},{128,96},{160,128},{192,160},{224,1... | collective-permute-start | bytes 147464 | tf_op jit(solution)/shard_map/ppermute | solution.py:34
  137.3 2.3 %collective-permute-start.11 = (f32[1,2,2,12,256]{4,3,2,1,0:T(8,128)S(1)}, f32[1,2,2,12,256]{4,3,2,1,0:T(8,128)S(1)}, u32[]{:S(2)}, u32[]{:S(2)}) collective-permute-start(f32[1,2,2,12,256]{4,3,2,1,0:T(8,128)S(1)} %get-tuple-element.161), channel_id=1, source_target_pairs={{0,32},{32,64},{64,96},{96,128},{128,160},{160,192},{192,224},{224... | collective-permute-start | bytes 147464 | tf_op jit(solution)/shard_map/ppermute | solution.py:34
  142.2 4.3 %collective-permute-done.11 = f32[1,2,2,12,256]{4,3,2,1,0:T(8,128)S(1)} collective-permute-done((f32[1,2,2,12,256]{4,3,2,1,0:T(8,128)S(1)}, f32[1,2,2,12,256]{4,3,2,1,0:T(8,128)S(1)}, u32[]{:S(2)}, u32[]{:S(2)}) %collective-permute-start.11) | collective-permute-done | bytes 49184 | tf_op jit(solution)/shard_map/ppermute | solution.py:34
  146.6 0.7 fusion.21
  (470 shorter events, 14.4 us)
Async XLA Ops:
  0.6 12.2 %copy-start.2 = (f32[2,2,72,256]{3,2,1,0:T(8,128)S(1)}, f32[2,2,72,256]{3,2,1,0:T(8,128)}, u32[]{:S(2)}) copy-start(f32[2,2,72,256]{3,2,1,0:T(8,128)} %param.3) | copy-start | bytes 884740
  2.3 19.6 %all-to-all-start = ((f32[1,96,256]{2,0,1:T(1,128)}), f32[1,96,256]{2,0,1:T(1,128)S(1)}, u32[]{:S(2)}, u32[]{:S(2)}) async-start(f32[1,96,256]{2,0,1:T(1,128)} %reshape.4009), calls=%async_computation | async-start | bytes 196608 | tf_op jit(solution)/shard_map/all_to_all | solution.py:148
  22.9 13.3 %all-to-all-start.1 = ((f32[32,3,256]{2,1,0:T(4,128)}), f32[32,3,256]{2,1,0:T(4,128)S(1)}, u32[]{:S(2)}, u32[]{:S(2)}) async-start(f32[32,3,256]{2,1,0:T(4,128)} %rev.6), calls=%async_computation.1 | async-start | bytes 262144 | tf_op jit(solution)/shard_map/all_to_all | solution.py:150
  40.8 31.5 %collective-permute-start.2 = (f32[1,2,1,24,256]{4,2,3,1,0:T(1,128)S(1)}, f32[1,2,1,24,256]{4,2,3,1,0:T(1,128)S(1)}, u32[]{:S(2)}, u32[]{:S(2)}) collective-permute-start(f32[1,2,1,24,256]{4,2,3,1,0:T(1,128)S(1)} %get-tuple-element.171), channel_id=1, source_target_pairs={{1,0},{2,1},{3,2},{0,3},{5,4},{6,5},{7,6},{4,7},{9,8},{10,9},{11,1... | collective-permute-start | bytes 147464 | tf_op jit(solution)/shard_map/ppermute | solution.py:26
  58.8 20.2 %collective-permute-start.3 = (f32[1,2,1,24,256]{4,2,3,1,0:T(1,128)S(1)}, f32[1,2,1,24,256]{4,2,3,1,0:T(1,128)S(1)}, u32[]{:S(2)}, u32[]{:S(2)}) collective-permute-start(f32[1,2,1,24,256]{4,2,3,1,0:T(1,128)S(1)} %get-tuple-element.170), channel_id=1, source_target_pairs={{0,1},{1,2},{2,3},{3,0},{4,5},{5,6},{6,7},{7,4},{8,9},{9,10},{10,1... | collective-permute-start | bytes 147464 | tf_op jit(solution)/shard_map/ppermute | solution.py:25
  61.6 18.1 %collective-permute-start = (f32[1,1,2,24,256]{4,2,3,1,0:T(2,128)S(1)}, f32[1,1,2,24,256]{4,2,3,1,0:T(2,128)S(1)}, u32[]{:S(2)}, u32[]{:S(2)}) collective-permute-start(f32[1,1,2,24,256]{4,2,3,1,0:T(2,128)S(1)} %get-tuple-element.183), channel_id=1, source_target_pairs={{4,0},{8,4},{12,8},{16,12},{20,16},{24,20},{28,24},{0,28},{5,1},{9... | collective-permute-start | bytes 147464 | tf_op jit(solution)/shard_map/ppermute | solution.py:26
  67.0 12.6 %collective-permute-start.1 = (f32[1,1,2,24,256]{4,2,3,1,0:T(2,128)S(1)}, f32[1,1,2,24,256]{4,2,3,1,0:T(2,128)S(1)}, u32[]{:S(2)}, u32[]{:S(2)}) collective-permute-start(f32[1,1,2,24,256]{4,2,3,1,0:T(2,128)S(1)} %get-tuple-element.182), channel_id=1, source_target_pairs={{0,4},{4,8},{8,12},{12,16},{16,20},{20,24},{24,28},{28,0},{1,5},{5... | collective-permute-start | bytes 147464 | tf_op jit(solution)/shard_map/ppermute | solution.py:25
  70.1 10.9 %collective-permute-start.5 = (f32[1,2,2,12,256]{4,3,2,1,0:T(8,128)S(1)}, f32[1,2,2,12,256]{4,3,2,1,0:T(8,128)S(1)}, u32[]{:S(2)}, u32[]{:S(2)}) collective-permute-start(f32[1,2,2,12,256]{4,3,2,1,0:T(8,128)S(1)} %get-tuple-element.189), channel_id=1, source_target_pairs={{0,32},{32,64},{64,96},{96,128},{128,160},{160,192},{192,224},{224... | collective-permute-start | bytes 147464 | tf_op jit(solution)/shard_map/ppermute | solution.py:34
  72.3 9.3 %collective-permute-start.4 = (f32[1,2,2,12,256]{4,3,2,1,0:T(8,128)S(1)}, f32[1,2,2,12,256]{4,3,2,1,0:T(8,128)S(1)}, u32[]{:S(2)}, u32[]{:S(2)}) collective-permute-start(f32[1,2,2,12,256]{4,3,2,1,0:T(8,128)S(1)} %get-tuple-element.188), channel_id=1, source_target_pairs={{0,992},{32,0},{64,32},{96,64},{128,96},{160,128},{192,160},{224,1... | collective-permute-start | bytes 147464 | tf_op jit(solution)/shard_map/ppermute | solution.py:34
  81.6 0.9 copy-start
  82.5 64.0 %copy-start.1 = (f32[1,2,2,24,256]{4,3,2,1,0:T(8,128)}, f32[1,2,2,24,256]{4,3,2,1,0:T(8,128)S(1)}, u32[]{:S(2)}) copy-start(f32[1,2,2,24,256]{4,3,2,1,0:T(8,128)S(1)} %fusion.11) | copy-start | bytes 294916
  115.4 21.9 %collective-permute-start.8 = (f32[1,2,1,24,256]{4,2,3,1,0:T(1,128)S(1)}, f32[1,2,1,24,256]{4,2,3,1,0:T(1,128)S(1)}, u32[]{:S(2)}, u32[]{:S(2)}) collective-permute-start(f32[1,2,1,24,256]{4,2,3,1,0:T(1,128)S(1)} %get-tuple-element.143), channel_id=1, source_target_pairs={{1,0},{2,1},{3,2},{0,3},{5,4},{6,5},{7,6},{4,7},{9,8},{10,9},{11,1... | collective-permute-start | bytes 147464 | tf_op jit(solution)/shard_map/ppermute | solution.py:26
  123.0 16.6 %collective-permute-start.9 = (f32[1,2,1,24,256]{4,2,3,1,0:T(1,128)S(1)}, f32[1,2,1,24,256]{4,2,3,1,0:T(1,128)S(1)}, u32[]{:S(2)}, u32[]{:S(2)}) collective-permute-start(f32[1,2,1,24,256]{4,2,3,1,0:T(1,128)S(1)} %get-tuple-element.142), channel_id=1, source_target_pairs={{0,1},{1,2},{2,3},{3,0},{4,5},{5,6},{6,7},{7,4},{8,9},{9,10},{10,1... | collective-permute-start | bytes 147464 | tf_op jit(solution)/shard_map/ppermute | solution.py:25
  125.5 14.7 %collective-permute-start.6 = (f32[1,1,2,24,256]{4,2,3,1,0:T(2,128)S(1)}, f32[1,1,2,24,256]{4,2,3,1,0:T(2,128)S(1)}, u32[]{:S(2)}, u32[]{:S(2)}) collective-permute-start(f32[1,1,2,24,256]{4,2,3,1,0:T(2,128)S(1)} %get-tuple-element.155), channel_id=1, source_target_pairs={{4,0},{8,4},{12,8},{16,12},{20,16},{24,20},{28,24},{0,28},{5,1},{9... | collective-permute-start | bytes 147464 | tf_op jit(solution)/shard_map/ppermute | solution.py:26
  131.0 9.3 %collective-permute-start.7 = (f32[1,1,2,24,256]{4,2,3,1,0:T(2,128)S(1)}, f32[1,1,2,24,256]{4,2,3,1,0:T(2,128)S(1)}, u32[]{:S(2)}, u32[]{:S(2)}) collective-permute-start(f32[1,1,2,24,256]{4,2,3,1,0:T(2,128)S(1)} %get-tuple-element.154), channel_id=1, source_target_pairs={{0,4},{4,8},{8,12},{12,16},{16,20},{20,24},{24,28},{28,0},{1,5},{5... | collective-permute-start | bytes 147464 | tf_op jit(solution)/shard_map/ppermute | solution.py:25
  134.3 7.4 %collective-permute-start.10 = (f32[1,2,2,12,256]{4,3,2,1,0:T(8,128)S(1)}, f32[1,2,2,12,256]{4,3,2,1,0:T(8,128)S(1)}, u32[]{:S(2)}, u32[]{:S(2)}) collective-permute-start(f32[1,2,2,12,256]{4,3,2,1,0:T(8,128)S(1)} %get-tuple-element.160), channel_id=1, source_target_pairs={{0,992},{32,0},{64,32},{96,64},{128,96},{160,128},{192,160},{224,1... | collective-permute-start | bytes 147464 | tf_op jit(solution)/shard_map/ppermute | solution.py:34
  137.3 9.2 %collective-permute-start.11 = (f32[1,2,2,12,256]{4,3,2,1,0:T(8,128)S(1)}, f32[1,2,2,12,256]{4,3,2,1,0:T(8,128)S(1)}, u32[]{:S(2)}, u32[]{:S(2)}) collective-permute-start(f32[1,2,2,12,256]{4,3,2,1,0:T(8,128)S(1)} %get-tuple-element.161), channel_id=1, source_target_pairs={{0,32},{32,64},{64,96},{96,128},{128,160},{160,192},{192,224},{224... | collective-permute-start | bytes 147464 | tf_op jit(solution)/shard_map/ppermute | solution.py:34
where the time goes:
time: 148 us; the launch traced here: 147 us
  starting transfers between devices  74.4 us (50%)
  blocking collectives  27.8 us (19%)
  waiting for transfers between devices  22 us (15%)
  local copies, waits for them, and re-layouts  9.42 us (6%)
  other arithmetic  9.3 us (6%)
  between operations  4.27 us (3%)
    ppermute x4, starting transfers between devices, padded(): after = lax.ppermute(first, axis, down)  36.4 us
    all_to_all x1, blocking collectives, mirror(): lax.all_to_all(flat, 'sa', split_axis=1, concat_axis=0, tiled=True)  15.2 us
    ppermute x4, starting transfers between devices, shifted(): return lax.ppermute(value, axis, pairs)  13.9 us
    all_to_all x1, blocking collectives, mirror(): lax.all_to_all(slab_rows, 'sa', split_axis=0, concat_axis=1, tiled=True)  12.6 us
    all_to_all x1, starting transfers between devices, mirror(): lax.all_to_all(flat, 'sa', split_axis=1, concat_axis=0, tiled=True)  10.5 us
    ppermute x4, starting transfers between devices, padded(): before = lax.ppermute(last, axis, up)  9.84 us
    all_to_all x1, waiting for transfers between devices, mirror(): lax.all_to_all(slab_rows, 'sa', split_axis=0, concat_axis=1, tiled=True)  9.38 us
    all_to_all x1, waiting for transfers between devices, mirror(): lax.all_to_all(flat, 'sa', split_axis=1, concat_axis=0, tiled=True)  8.28 us
  transfers between devices with their start and end apart: 14, of which 3 were waited for; matrix products, arithmetic and copies ran while one was open for 4% of the time, Pallas kernels for 0%

commit v1 on v0

v1 whole, which is shorter than its diff:
```python
import functools

import jax
import jax.numpy as jnp
from jax import lax
from jax.experimental import pallas as pl
from jax.experimental.pallas import tpu as pltpu
from jax.sharding import PartitionSpec as P

MESH = pl.DeviceIdType.MESH

m5_height = 1.8
wall_mass = 0.1
cheb_scale = 0.2
cheb_shift = -0.5
diagonal = 5.0 - m5_height
source = ((3, 2), (3, 2), (2, 3), (2, 3))
coefficient = (
    ((0, -1), (0, -1), (0, 1), (0, 1)),
    ((-1, 0), (1, 0), (1, 0), (-1, 0)),
    ((0, -1), (0, 1), (0, 1), (0, -1)),
    ((1, 0), (1, 0), (1, 0), (1, 0)),
)
STRIDE = (2, 1)

GY_UP, GY_DOWN, GX_UP, GX_DOWN, SA_UP, SA_DOWN, MIRROR = range(7)


def add_times(base, coef, value):
    re, im = value
    if coef[0] == 1:
        return base[0] + re, base[1] + im
    if coef[0] == -1:
        return base[0] - re, base[1] - im
    if coef[1] == 1:
        return base[0] - im, base[1] + re
    return base[0] + im, base[1] - re


def scaled(coef, sign):
    return coef[0] * sign, coef[1] * sign


def project(field, direction, sign):
    parts = [
        add_times(field(a), scaled(coefficient[direction][a], sign), field(source[direction][a]))
        for a in range(2)
    ]
    return jnp.stack([p[0] for p in parts]), jnp.stack([p[1] for p in parts])


def expand(total, half, direction, sign):
    total = list(total)
    for a in range(2):
        b = source[direction][a]
        value = (half[0][a], half[1][a])
        total[a] = (total[a][0] + value[0], total[a][1] + value[1])
        total[b] = add_times(total[b], scaled(coefficient[direction][b], sign), value)
    return total


def link_of(links, direction):
    base = direction * 18
    re = links[base : base + 9].reshape(3, 3, 8, 128)
    im = links[base + 9 : base + 18].reshape(3, 3, 8, 128)
    return re, im


def link_times(link, half, adjoint):
    re, im = None, None
    for j in range(3):
        u_re = (link[0][j] if adjoint else link[0][:, j])[None]
        u_im = (link[1][j] if adjoint else link[1][:, j])[None]
        h_re, h_im = half[0][:, j][:, None], half[1][:, j][:, None]
        if adjoint:
            t_re = u_re * h_re + u_im * h_im
            t_im = u_re * h_im - u_im * h_re
        else:
            t_re = u_re * h_re - u_im * h_im
            t_im = u_re * h_im + u_im * h_re
        re = t_re if re is None else re + t_re
        im = t_im if im is None else im + t_im
    return re, im


def rolled(value, shift, axis):
    size = value.shape[axis]
    flat = value.reshape((-1,) + value.shape[-2:])
    return pltpu.roll(flat, shift % size, axis + 3).reshape(value.shape)


def masks():
    lane = lax.broadcasted_iota(jnp.int32, (1, 1, 8, 128), 3)
    sub = lax.broadcasted_iota(jnp.int32, (1, 1, 8, 128), 2)
    time = lane % 64
    return {
        "first": time == 0,
        "last": time == 63,
        "zlow": lane < 64,
        "low": tuple((sub // q) % 2 == 0 for q in STRIDE),
    }


def ahead_local(half, direction, mask):
    out = []
    for value in half:
        if direction == 2:
            near = rolled(value, 64, -1)
            out.append(jnp.where(mask["zlow"], near, rolled(near, 4, -2)))
        else:
            out.append(jnp.where(mask["last"], -rolled(value, 63, -1), rolled(value, -1, -1)))
    return out


def behind_local(half, direction, mask):
    out = []
    for value in half:
        if direction == 2:
            near = rolled(value, 64, -1)
            out.append(jnp.where(mask["zlow"], rolled(near, 4, -2), near))
        else:
            out.append(jnp.where(mask["first"], -rolled(value, -63, -1), rolled(value, 1, -1)))
    return out


def kernel(
    v_hbm,
    u_hbm,
    once_ref,
    twice_ref,
    vin,
    uin,
    field_v,
    links,
    field_g,
    mirror_out,
    mirror_in,
    face_out,
    face_in,
    chiral_in,
    local_sem,
    send_sem,
    recv_sem,
):
    axes = ("sa", "gx", "gy")
    me = {axis: lax.axis_index(axis) for axis in axes}
    size = {axis: lax.axis_size(axis) for axis in axes}

    def step(axis, by):
        return {axis: lax.rem(me[axis] + by + size[axis], size[axis])}

    target = {
        GY_UP: step("gy", 1),
        GY_DOWN: step("gy", -1),
        GX_UP: step("gx", 1),
        GX_DOWN: step("gx", -1),
        SA_UP: step("sa", 1),
        SA_DOWN: step("sa", -1),
        MIRROR: {"sa": size["sa"] - 1 - me["sa"]},
    }
    barrier = pltpu.get_barrier_semaphore()
    for device in target.values():
        pl.semaphore_signal(barrier, inc=1, device_id=device, device_id_type=MESH)

    loads = []
    for h in range(2):
        lanes = pl.ds(128 * h, 128)
        loads.append(
            pltpu.make_async_copy(v_hbm.at[:, lanes], vin.at[pl.ds(96 * h, 96)], local_sem.at[h])
        )
        loads.append(
            pltpu.make_async_copy(
                u_hbm.at[:, lanes], uin.at[pl.ds(288 * h, 288)], local_sem.at[2 + h]
            )
        )
    for load in loads:
        load.start()
    for load in loads:
        load.wait()

    for r in range(24):
        field_v[r] = vin[pl.ds(r, 8, stride=24), :]
    for r in range(72):
        links[r] = uin[pl.ds(r, 8, stride=72), :]

    mask = masks()
    copies = {}

    def send(stage, way, src, dst):
        index = stage * 7 + way
        copy = pltpu.make_async_remote_copy(
            src_ref=src,
            dst_ref=dst,
            send_sem=send_sem.at[index],
            recv_sem=recv_sem.at[index],
            device_id=target[way],
            device_id_type=MESH,
        )
        copies[stage, way] = copy
        copy.start()

    def reader(ref):
        def spin(a):
            return ref[a * 6 : a * 6 + 3], ref[a * 6 + 3 : a * 6 + 6]

        return spin

    def faces(field, direction, sign, stage):
        q = STRIDE[direction]
        low = mask["low"][direction]
        up, down = ((GX_UP, GX_DOWN), (GY_UP, GY_DOWN))[direction]
        ahead = project(field, direction, -sign)
        packed = jnp.where(low, ahead[0], rolled(ahead[1], q, -2))
        face_out[stage * 4 + down] = packed.reshape(6, 8, 128)
        behind = link_times(link_of(links, direction), project(field, direction, sign), True)
        packed = jnp.where(low, rolled(behind[1], -q, -2), behind[0])
        face_out[stage * 4 + up] = packed.reshape(6, 8, 128)
        return ahead, behind

    def send_faces(direction, stage):
        for way in ((GX_DOWN, GX_UP), (GY_DOWN, GY_UP))[direction]:
            send(stage, way, face_out.at[stage * 4 + way], face_in.at[stage * 4 + way])

    def hops_local(total, field, sign):
        for direction in (2, 3):
            link = link_of(links, direction)
            ahead = ahead_local(project(field, direction, -sign), direction, mask)
            total = expand(total, link_times(link, ahead, False), direction, -sign)
            behind = link_times(link, project(field, direction, sign), True)
            total = expand(total, behind_local(behind, direction, mask), direction, sign)
        return total

    def hops_across(total, local, direction, sign, stage):
        q = STRIDE[direction]
        low = mask["low"][direction]
        up, down = ((GX_UP, GX_DOWN), (GY_UP, GY_DOWN))[direction]
        ahead, behind = local
        copies[stage, down].wait_recv()
        halo = face_in[stage * 4 + down].reshape(2, 3, 8, 128)
        ahead = (
            jnp.where(low, rolled(ahead[0], -q, -2), rolled(halo, q, -2)),
            jnp.where(low, rolled(ahead[1], -q, -2), halo),
        )
        total = expand(
            total, link_times(link_of(links, direction), ahead, False), direction, -sign
        )
        copies[stage, up].wait_recv()
        halo = face_in[stage * 4 + up].reshape(2, 3, 8, 128)
        behind = (
            jnp.where(low, rolled(halo, -q, -2), rolled(behind[0], q, -2)),
            jnp.where(low, halo, rolled(behind[1], q, -2)),
        )
        return expand(total, behind, direction, sign)

    zero = jnp.zeros((3, 8, 128), jnp.float32)
    nothing = [(zero, zero)] * 4
    last = size["sa"] - 1
    from_down = jnp.where(me["sa"] == 0, -wall_mass, 1.0).astype(jnp.float32)
    from_up = jnp.where(me["sa"] == last, -wall_mass, 1.0).astype(jnp.float32)

    field = reader(field_v)
    local_y = faces(field, 1, 1, 0)
    local_x = faces(field, 0, 1, 0)
    pl.semaphore_wait(barrier, 7)
    send_faces(1, 0)
    send_faces(0, 0)
    send(0, SA_UP, field_v.at[pl.ds(0, 12)], chiral_in.at[pl.ds(0, 12)])
    send(0, SA_DOWN, field_v.at[pl.ds(12, 12)], chiral_in.at[pl.ds(12, 12)])
    total = hops_local(nothing, field, 1)
    total = hops_across(total, local_x, 0, 1, 0)
    total = hops_across(total, local_y, 1, 1, 0)
    copies[0, SA_UP].wait_recv()
    copies[0, SA_DOWN].wait_recv()
    for a in range(4):
        scale = from_down if a < 2 else from_up
        for part in range(2):
            row = a * 6 + part * 3
            value = (
                diagonal * field_v[row : row + 3]
                - 0.5 * total[a][part]
                - scale * chiral_in[row : row + 3]
            )
            field_g[row : row + 3] = value
            for c in range(3):
                mirror_out[pl.ds(row + c, 8, stride=24), :] = value[c]

    send(1, SA_DOWN, field_g.at[pl.ds(0, 12)], chiral_in.at[pl.ds(24, 12)])
    send(1, SA_UP, field_g.at[pl.ds(12, 12)], chiral_in.at[pl.ds(36, 12)])
    send(1, MIRROR, mirror_out, mirror_in)
    field = reader(field_g)
    local_y = faces(field, 1, -1, 1)
    send_faces(1, 1)
    local_x = faces(field, 0, -1, 1)
    send_faces(0, 1)
    total = hops_local(nothing, field, -1)
    total = hops_across(total, local_x, 0, -1, 1)
    total = hops_across(total, local_y, 1, -1, 1)
    copies[1, SA_DOWN].wait_recv()
    copies[1, SA_UP].wait_recv()
    second = 2.0 * cheb_scale * cheb_scale
    for a in range(4):
        scale = from_up if a < 2 else from_down
        for part in range(2):
            row = a * 6 + part * 3
            value = second * (
                diagonal * field_g[row : row + 3]
                - 0.5 * total[a][part]
                - scale * chiral_in[24 + row : 24 + row + 3]
            )
            value = value - 0.5 * field_v[row : row + 3]
            for c in range(3):
                mirror_out_row = pl.ds(row + c, 8, stride=24)
                uin[mirror_out_row, :] = value[c]
    copies[1, MIRROR].wait_recv()
    rows = lax.broadcasted_iota(jnp.int32, (24, 128), 0)
    five = jnp.where(rows < 12, cheb_scale, -cheb_scale).astype(jnp.float32)
    for site in range(4):
        for h in range(2):
            block = pl.ds(h * 96 + site * 24, 24)
            hv = five * mirror_in[block, :]
            place = (pl.ds(site * 24, 24), pl.ds(128 * h, 128))
            once_ref[place] = hv + cheb_shift * vin[block, :]
            twice_ref[place] = uin[block, :] - 2.0 * hv
    for copy in copies.values():
        copy.wait_send()


def per_device(vectors, gauge_links):
    field = vectors.reshape(96, 256)
    links = gauge_links.reshape(288, 256)
    shape = jax.ShapeDtypeStruct((96, 256), jnp.float32)
    once, twice = pl.pallas_call(
        kernel,
        out_shape=(shape, shape),
        in_specs=[pl.BlockSpec(memory_space=pl.ANY)] * 2,
        out_specs=[pl.BlockSpec(memory_space=pltpu.VMEM)] * 2,
        scratch_shapes=[
            pltpu.VMEM((192, 128), jnp.float32),
            pltpu.VMEM((576, 128), jnp.float32),
            pltpu.VMEM((24, 8, 128), jnp.float32),
            pltpu.VMEM((72, 8, 128), jnp.float32),
            pltpu.VMEM((24, 8, 128), jnp.float32),
            pltpu.VMEM((192, 128), jnp.float32),
            pltpu.VMEM((192, 128), jnp.float32),
            pltpu.VMEM((8, 6, 8, 128), jnp.float32),
            pltpu.VMEM((8, 6, 8, 128), jnp.float32),
            pltpu.VMEM((48, 8, 128), jnp.float32),
            pltpu.SemaphoreType.DMA((4,)),
            pltpu.SemaphoreType.DMA((14,)),
            pltpu.SemaphoreType.DMA((14,)),
        ],
        compiler_params=pltpu.CompilerParams(collective_id=0, has_side_effects=True),
        name="chebyshev",
    )(field, links)
    return once.reshape(vectors.shape), twice.reshape(vectors.shape)


def solution(mesh):
    placed = (P("sa", "gx", "gy", None, None), P("gx", "gy", None, None))
    return jax.shard_map(
        per_device,
        mesh=mesh,
        in_specs=placed,
        out_specs=(placed[0], placed[0]),
        check_vma=False,
    )
```

time: 148 us -> 37.8 us (0.26)
  starting transfers between devices: 74.4 us -> 0 us
  Pallas kernels: 0 us -> 34.8 us
  blocking collectives: 27.8 us -> 0 us
  waiting for transfers between devices: 22 us -> 0 us
  other arithmetic: 9.3 us -> 0 us
  local copies, waits for them, and re-layouts: 9.42 us -> 2.22 us
  between operations: 4.27 us -> 0.65 us
    ppermute x12 -> x0, starting transfers between devices: 60.1 us -> none  [the longest x4 36.4 us: padded(): after = lax.ppermute(first, axis, down)]
    pallas_call x0 -> x1, Pallas kernels: none -> 34.8 us  [per_device(): pl.pallas_call(kernel, out_shape=(shape, shape), in_specs=[pl.BlockSpec(m...]
    all_to_all x2 -> x0, blocking collectives: 27.8 us -> none  [the longest x1 15.2 us: mirror(): lax.all_to_all(flat, 'sa', split_axis=1, concat_axis=0, tiled=True)]
    all_to_all x2 -> x0, waiting for transfers between devices: 17.7 us -> none  [the longest x1 9.38 us: mirror(): lax.all_to_all(slab_rows, 'sa', split_axis=0, concat_axis=1, tiled=True)]
    all_to_all x2 -> x0, starting transfers between devices: 14.3 us -> none  [the longest x1 10.5 us: mirror(): lax.all_to_all(flat, 'sa', split_axis=1, concat_axis=0, tiled=True)]
    ppermute x12 -> x0, waiting for transfers between devices: 4.36 us -> none  [the longest x4 4.33 us: shifted(): return lax.ppermute(value, axis, pairs)]
    slice x64 -> x0, local copies, waits for them, and re-layouts: 2.06 us -> none  [the longest x4 0.46 us: along_local(): jnp.roll(spinor, 1 - NT, axis=-1)]
    reshape x4 -> x0, local copies, waits for them, and re-layouts: 1.88 us -> none  [the longest x2 1.78 us: mirror(): spinor.reshape(spinor.shape[0], spinor.shape[1] * spinor.shape[2] * spino...]
  transfers between devices with their start and end apart: 14 -> 0, of which waited for: 3 -> 0; matrix products, arithmetic and copies ran while one was open for 4% -> 0% of each run, Pallas kernels for 0% -> 0%
where the time goes in v1:
time: 37.8 us; the launch traced here: 37.6 us
  Pallas kernels  34.8 us (92%)
  local copies, waits for them, and re-layouts  2.22 us (6%)
  between operations  0.65 us (2%)
    pallas_call x1, Pallas kernels, per_device(): pl.pallas_call(kernel, out_shape=(shape, shape), in_specs=[pl.BlockSpec(m...  34.8 us
    unnamed x4, local copies, waits for them, and re-layouts  2.22 us

profile of v1, /device:TPU:1, one launch (start us, length us, event | category | flops | bytes accessed | tf_op | source)
XLA Modules:
  0.0 37.6 jit_solution(14630692458927707231)
XLA Ops:
  0.6 34.8 %chebyshev.1 = (f32[96,256]{1,0:T(8,128)}, f32[96,256]{1,0:T(8,128)}) custom-call(f32[96,256]{1,0:T(8,128)} %bitcast.7, f32[288,256]{1,0:T(8,128)} %bitcast.4), custom_call_target="tpu_custom_call" | custom-call | tf_op jit(solution)/shard_map/chebyshev/pallas_call | solution.py:332
  35.4 0.0 copy-start
  35.4 1.6 %copy.6 = f32[1,2,2,24,256]{4,3,2,1,0:T(8,128)} copy(f32[1,2,2,24,256]{4,3,2,1,0:T(8,128)} %bitcast.6) | data formatting | bytes 196608
  37.0 0.0 copy-done
  37.0 0.6 %copy.7 = f32[1,2,2,24,256]{4,3,2,1,0:T(8,128)} copy(f32[1,2,2,24,256]{4,3,2,1,0:T(8,128)S(1)} %bitcast.5) | data formatting | bytes 196608
Async XLA Ops:
  35.4 1.6 %copy-start = (f32[96,256]{1,0:T(8,128)S(1)}, f32[96,256]{1,0:T(8,128)}, u32[]{:S(2)}) copy-start(f32[96,256]{1,0:T(8,128)} %get-tuple-element.5) | copy-start | bytes 294916

commit v2 on v1

--- a/solution.py
+++ b/solution.py
@@ -319,8 +319,8 @@
             block = pl.ds(h * 96 + site * 24, 24)
             hv = five * mirror_in[block, :]
             place = (pl.ds(site * 24, 24), pl.ds(128 * h, 128))
-            once_ref[place] = hv + cheb_shift * vin[block, :]
-            twice_ref[place] = uin[block, :] - 2.0 * hv
+            once_ref[place] = hv
+            twice_ref[place] = uin[block, :]
     for copy in copies.values():
         copy.wait_send()
 
@@ -328,7 +328,7 @@
 def per_device(vectors, gauge_links):
     field = vectors.reshape(96, 256)
     links = gauge_links.reshape(288, 256)
-    shape = jax.ShapeDtypeStruct((96, 256), jnp.float32)
+    shape = pltpu.VMEM((96, 256), jnp.float32)
     once, twice = pl.pallas_call(
         kernel,
         out_shape=(shape, shape),
@@ -352,6 +352,9 @@
         compiler_params=pltpu.CompilerParams(collective_id=0, has_side_effects=True),
         name="chebyshev",
     )(field, links)
+    hv, rest = once, twice
+    once = hv + cheb_shift * field
+    twice = rest - 2.0 * hv
     return once.reshape(vectors.shape), twice.reshape(vectors.shape)
 
 

time: 37.8 us -> 35.7 us (0.944)
  local copies, waits for them, and re-layouts: 2.22 us -> 0.01 us
  other arithmetic: 0 us -> 0.69 us
  Pallas kernels: 34.8 us -> 34.2 us
    unnamed x4 -> x2, local copies, waits for them, and re-layouts: 2.22 us -> 0.01 us
    sub x0 -> x1, other arithmetic: none -> 0.69 us  [per_device(): twice = rest - 2.0 * hv]
    pallas_call x1, Pallas kernels: 34.8 us -> 34.2 us  [per_device(): pl.pallas_call(kernel, out_shape=(shape, shape), in_specs=[pl.BlockSpec(m...]
where the time goes in v2:
time: 35.7 us; the launch traced here: 35.6 us
  Pallas kernels  34.2 us (96%)
  other arithmetic  0.69 us (2%)
  between operations  0.65 us (2%)
    pallas_call x1, Pallas kernels, per_device(): pl.pallas_call(kernel, out_shape=(shape, shape), in_specs=[pl.BlockSpec(m...  34.2 us

profile of v2, /device:TPU:1, one launch (start us, length us, event | category | flops | bytes accessed | tf_op | source)
XLA Modules:
  0.0 35.6 jit_solution(14998770904118495479)
XLA Ops:
  0.6 0.0 copy-start
  0.6 34.2 %chebyshev.1 = (f32[96,256]{1,0:T(8,128)S(1)}, f32[96,256]{1,0:T(8,128)S(1)}) custom-call(f32[96,256]{1,0:T(8,128)} %bitcast.5, f32[288,256]{1,0:T(8,128)} %bitcast.6), custom_call_target="tpu_custom_call" | custom-call | tf_op jit(solution)/shard_map/chebyshev/pallas_call | solution.py:332
  34.9 0.0 copy-done
  34.9 0.7 %multiply_subtract_fusion = (f32[96,256]{1,0:T(8,128)}, f32[96,256]{1,0:T(8,128)}) fusion(f32[96,256]{1,0:T(8,128)S(1)} %get-tuple-element.5, f32[96,256]{1,0:T(8,128)S(1)} %get-tuple-element.4, f32[1,2,2,24,256]{4,3,2,1,0:T(8,128)S(1)} %copy-done), kind=kLoop, calls=%fused_computation | loop fusion | flops 98304 | bytes 491520 | tf_op jit(solution)/shard_map/sub | solution.py:357
Async XLA Ops:
  0.6 34.2 %copy-start = (f32[1,2,2,24,256]{4,3,2,1,0:T(8,128)S(1)}, f32[1,2,2,24,256]{4,3,2,1,0:T(8,128)}, u32[]{:S(2)}) copy-start(f32[1,2,2,24,256]{4,3,2,1,0:T(8,128)} %param.2) | copy-start | bytes 294916

commit v3 on v2

--- a/solution.py
+++ b/solution.py
@@ -24,6 +24,8 @@
 STRIDE = (2, 1)
 
 GY_UP, GY_DOWN, GX_UP, GX_DOWN, SA_UP, SA_DOWN, MIRROR = range(7)
+BACK = (GY_DOWN, GY_UP, GX_DOWN, GX_UP, SA_DOWN, SA_UP, MIRROR)
+MAIN, RELAY_UP, RELAY_DOWN = 12, 13, 14
 
 
 def add_times(base, coef, value):
@@ -126,19 +128,22 @@
 def kernel(
     v_hbm,
     u_hbm,
-    once_ref,
-    twice_ref,
+    mirrored_ref,
+    rest_ref,
     vin,
     uin,
     field_v,
     links,
+    field_p,
     field_g,
-    mirror_out,
-    mirror_in,
     face_out,
     face_in,
     chiral_in,
+    mirror_in,
+    relay_in,
+    natural,
     local_sem,
+    known_sem,
     send_sem,
     recv_sem,
 ):
@@ -149,18 +154,34 @@
     def step(axis, by):
         return {axis: lax.rem(me[axis] + by + size[axis], size[axis])}
 
-    target = {
-        GY_UP: step("gy", 1),
-        GY_DOWN: step("gy", -1),
-        GX_UP: step("gx", 1),
-        GX_DOWN: step("gx", -1),
-        SA_UP: step("sa", 1),
-        SA_DOWN: step("sa", -1),
-        MIRROR: {"sa": size["sa"] - 1 - me["sa"]},
-    }
+    target = (
+        step("gy", 1),
+        step("gy", -1),
+        step("gx", 1),
+        step("gx", -1),
+        step("sa", 1),
+        step("sa", -1),
+        {"sa": size["sa"] - 1 - me["sa"]},
+    )
+
+    def rank(axis, index):
+        return index + 1 - 2 * lax.rem(index, 2) if axis == "gx" else index
+
+    first = []
+    lowest = me["gy"] == 0
+    for way, device in enumerate(target):
+        ((axis, index),) = device.items()
+        ahead = rank(axis, me[axis]) < rank(axis, index)
+        if way in (SA_UP, SA_DOWN):
+            wraps = jnp.abs(me[axis] - index) == size[axis] - 1
+            ahead = jnp.logical_xor(ahead, jnp.logical_and(lowest, wraps))
+        first.append(ahead)
     barrier = pltpu.get_barrier_semaphore()
-    for device in target.values():
-        pl.semaphore_signal(barrier, inc=1, device_id=device, device_id_type=MESH)
+    for way, device in enumerate(target):
+
+        @pl.when(first[way])
+        def _(device=device):
+            pl.semaphore_signal(barrier, inc=1, device_id=device, device_id_type=MESH)
 
     loads = []
     for h in range(2):
@@ -175,20 +196,11 @@
         )
     for load in loads:
         load.start()
-    for load in loads:
-        load.wait()
-
-    for r in range(24):
-        field_v[r] = vin[pl.ds(r, 8, stride=24), :]
-    for r in range(72):
-        links[r] = uin[pl.ds(r, 8, stride=72), :]
-
-    mask = masks()
+
     copies = {}
 
-    def send(stage, way, src, dst):
-        index = stage * 7 + way
-        copy = pltpu.make_async_remote_copy(
+    def copy_of(index, way, src, dst):
+        copies[index] = pltpu.make_async_remote_copy(
             src_ref=src,
             dst_ref=dst,
             send_sem=send_sem.at[index],
@@ -196,8 +208,29 @@
             device_id=target[way],
             device_id_type=MESH,
         )
-        copies[stage, way] = copy
-        copy.start()
+        return copies[index]
+
+    def meet(way):
+        @pl.when(first[way])
+        def _():
+            pl.semaphore_wait(known_sem.at[way], 1)
+
+    for stage in range(2):
+        for way in (GY_UP, GY_DOWN, GX_UP, GX_DOWN):
+            slot = stage * 4 + way
+            copy_of(stage * 6 + way, way, face_out.at[slot], face_in.at[slot])
+    upper, lower = pl.ds(0, 12), pl.ds(12, 12)
+    copy_of(SA_UP, SA_UP, field_v.at[upper], chiral_in.at[pl.ds(0, 12)])
+    copy_of(SA_DOWN, SA_DOWN, field_v.at[lower], chiral_in.at[pl.ds(12, 12)])
+    copy_of(6 + SA_DOWN, SA_DOWN, field_g.at[upper], chiral_in.at[pl.ds(24, 12)])
+    copy_of(6 + SA_UP, SA_UP, field_g.at[lower], chiral_in.at[pl.ds(36, 12)])
+    copy_of(MAIN, MIRROR, field_p, mirror_in)
+    copy_of(RELAY_UP, MIRROR, face_in.at[GY_DOWN], relay_in.at[0])
+    copy_of(RELAY_DOWN, MIRROR, face_in.at[GY_UP], relay_in.at[1])
+
+    mask = masks()
+    zero = jnp.zeros((3, 8, 128), jnp.float32)
+    nothing = [(zero, zero)] * 4
 
     def reader(ref):
         def spin(a):
@@ -205,21 +238,26 @@
 
         return spin
 
-    def faces(field, direction, sign, stage):
+    def halves(field, direction, sign):
+        ahead = project(field, direction, -sign)
+        behind = link_times(link_of(links, direction), project(field, direction, sign), True)
+        return ahead, behind
+
+    def pack(pair, direction, stage):
         q = STRIDE[direction]
         low = mask["low"][direction]
         up, down = ((GX_UP, GX_DOWN), (GY_UP, GY_DOWN))[direction]
-        ahead = project(field, direction, -sign)
+        ahead, behind = pair
         packed = jnp.where(low, ahead[0], rolled(ahead[1], q, -2))
         face_out[stage * 4 + down] = packed.reshape(6, 8, 128)
-        behind = link_times(link_of(links, direction), project(field, direction, sign), True)
         packed = jnp.where(low, rolled(behind[1], -q, -2), behind[0])
         face_out[stage * 4 + up] = packed.reshape(6, 8, 128)
-        return ahead, behind
-
-    def send_faces(direction, stage):
-        for way in ((GX_DOWN, GX_UP), (GY_DOWN, GY_UP))[direction]:
-            send(stage, way, face_out.at[stage * 4 + way], face_in.at[stage * 4 + way])
+
+    def unpack(from_up, from_down, direction):
+        q = STRIDE[direction]
+        from_up = from_up.reshape(2, 3, 8, 128)
+        from_down = from_down.reshape(2, 3, 8, 128)
+        return (rolled(from_up, q, -2), from_up), (rolled(from_down, -q, -2), from_down)
 
     def hops_local(total, field, sign):
         for direction in (2, 3):
@@ -230,74 +268,135 @@
             total = expand(total, behind_local(behind, direction, mask), direction, sign)
         return total
 
-    def hops_across(total, local, direction, sign, stage):
+    def hops_across(total, pair, halo, direction, sign):
         q = STRIDE[direction]
         low = mask["low"][direction]
-        up, down = ((GX_UP, GX_DOWN), (GY_UP, GY_DOWN))[direction]
-        ahead, behind = local
-        copies[stage, down].wait_recv()
-        halo = face_in[stage * 4 + down].reshape(2, 3, 8, 128)
-        ahead = (
-            jnp.where(low, rolled(ahead[0], -q, -2), rolled(halo, q, -2)),
-            jnp.where(low, rolled(ahead[1], -q, -2), halo),
-        )
-        total = expand(
-            total, link_times(link_of(links, direction), ahead, False), direction, -sign
-        )
-        copies[stage, up].wait_recv()
-        halo = face_in[stage * 4 + up].reshape(2, 3, 8, 128)
-        behind = (
-            jnp.where(low, rolled(halo, -q, -2), rolled(behind[0], q, -2)),
-            jnp.where(low, halo, rolled(behind[1], q, -2)),
-        )
+        ahead, behind = pair
+        ahead = [jnp.where(low, rolled(ahead[k], -q, -2), halo[0][k]) for k in range(2)]
+        behind = [jnp.where(low, halo[1][k], rolled(behind[k], q, -2)) for k in range(2)]
+        link = link_of(links, direction)
+        total = expand(total, link_times(link, ahead, False), direction, -sign)
         return expand(total, behind, direction, sign)
 
-    zero = jnp.zeros((3, 8, 128), jnp.float32)
-    nothing = [(zero, zero)] * 4
+    def halo_terms(halo):
+        low = mask["low"][1]
+        ahead = [jnp.where(low, 0.0, halo[0][k]) for k in range(2)]
+        behind = [jnp.where(low, halo[1][k], 0.0) for k in range(2)]
+        total = expand(nothing, link_times(link_of(links, 1), ahead, False), 1, -1)
+        return expand(total, behind, 1, 1)
+
     last = size["sa"] - 1
     from_down = jnp.where(me["sa"] == 0, -wall_mass, 1.0).astype(jnp.float32)
     from_up = jnp.where(me["sa"] == last, -wall_mass, 1.0).astype(jnp.float32)
+    no_halo = ((0.0, 0.0), (0.0, 0.0))
+
+    for load in loads:
+        load.wait()
+    for r in range(24):
+        field_v[r] = vin[pl.ds(r, 8, stride=24), :]
+    for r in range(72):
+        links[r] = uin[pl.ds(r, 8, stride=72), :]
 
     field = reader(field_v)
-    local_y = faces(field, 1, 1, 0)
-    local_x = faces(field, 0, 1, 0)
-    pl.semaphore_wait(barrier, 7)
-    send_faces(1, 0)
-    send_faces(0, 0)
-    send(0, SA_UP, field_v.at[pl.ds(0, 12)], chiral_in.at[pl.ds(0, 12)])
-    send(0, SA_DOWN, field_v.at[pl.ds(12, 12)], chiral_in.at[pl.ds(12, 12)])
+    pair_y = halves(field, 1, 1)
+    pack(pair_y, 1, 0)
+    pair_x = halves(field, 0, 1)
+    pack(pair_x, 0, 0)
+
+    count = jnp.int32(0)
+    for way in range(7):
+        count = count + jnp.where(first[way], 0, 1)
+    pl.semaphore_wait(barrier, count)
+    for way in (GY_UP, GY_DOWN):
+
+        @pl.when(jnp.logical_not(first[way]))
+        def _(way=way):
+            copies[way].start()
+
+    for way, device in enumerate(target):
+
+        @pl.when(jnp.logical_not(first[way]))
+        def _(way=way, device=device):
+            pl.semaphore_signal(
+                known_sem.at[BACK[way]], inc=1, device_id=device, device_id_type=MESH
+            )
+
+    for way in (GX_DOWN, GX_UP, SA_UP, SA_DOWN):
+        meet(way)
+        copies[way].start()
     total = hops_local(nothing, field, 1)
-    total = hops_across(total, local_x, 0, 1, 0)
-    total = hops_across(total, local_y, 1, 1, 0)
-    copies[0, SA_UP].wait_recv()
-    copies[0, SA_DOWN].wait_recv()
+    total = hops_across(total, pair_y, no_halo, 1, 1)
+    copies[GX_DOWN].wait_recv()
+    copies[GX_UP].wait_recv()
+    halo = unpack(face_in[GX_DOWN], face_in[GX_UP], 0)
+    total = hops_across(total, pair_x, halo, 0, 1)
+    copies[SA_UP].wait_recv()
+    copies[SA_DOWN].wait_recv()
     for a in range(4):
         scale = from_down if a < 2 else from_up
         for part in range(2):
             row = a * 6 + part * 3
-            value = (
+            field_p[row : row + 3] = (
                 diagonal * field_v[row : row + 3]
                 - 0.5 * total[a][part]
                 - scale * chiral_in[row : row + 3]
             )
-            field_g[row : row + 3] = value
-            for c in range(3):
-                mirror_out[pl.ds(row + c, 8, stride=24), :] = value[c]
-
-    send(1, SA_DOWN, field_g.at[pl.ds(0, 12)], chiral_in.at[pl.ds(24, 12)])
-    send(1, SA_UP, field_g.at[pl.ds(12, 12)], chiral_in.at[pl.ds(36, 12)])
-    send(1, MIRROR, mirror_out, mirror_in)
+    meet(MIRROR)
+    copies[MAIN].start()
+    pack(halves(reader(field_p), 1, -1), 1, 1)
+    for way in (GY_UP, GY_DOWN):
+
+        @pl.when(jnp.logical_not(first[way]))
+        def _(way=way):
+            copies[6 + way].start()
+
+    for way, relay in ((GY_UP, RELAY_UP), (GY_DOWN, RELAY_DOWN)):
+
+        @pl.when(first[way])
+        def _(way=way):
+            pl.semaphore_wait(known_sem.at[way], 1)
+            copies[way].start()
+            copies[6 + way].start()
+
+        copies[BACK[way]].wait_recv()
+        copies[relay].start()
+
+    halo = unpack(face_in[GY_DOWN], face_in[GY_UP], 1)
+    total = halo_terms(halo)
+    for a in range(4):
+        for part in range(2):
+            row = a * 6 + part * 3
+            field_g[row : row + 3] = field_p[row : row + 3] - 0.5 * total[a][part]
+    copies[6 + SA_DOWN].start()
+    copies[6 + SA_UP].start()
     field = reader(field_g)
-    local_y = faces(field, 1, -1, 1)
-    send_faces(1, 1)
-    local_x = faces(field, 0, -1, 1)
-    send_faces(0, 1)
+    pair_x = halves(field, 0, -1)
+    pack(pair_x, 0, 1)
+    copies[6 + GX_DOWN].start()
+    copies[6 + GX_UP].start()
     total = hops_local(nothing, field, -1)
-    total = hops_across(total, local_x, 0, -1, 1)
-    total = hops_across(total, local_y, 1, -1, 1)
-    copies[1, SA_DOWN].wait_recv()
-    copies[1, SA_UP].wait_recv()
+    copies[6 + GY_DOWN].wait_recv()
+    copies[6 + GY_UP].wait_recv()
+    halo = unpack(face_in[4 + GY_DOWN], face_in[4 + GY_UP], 1)
+    halo = (
+        [halo[0][k] - pair_y[1][k] for k in range(2)],
+        [halo[1][k] - pair_y[0][k] for k in range(2)],
+    )
+    total = hops_across(total, halves(field, 1, -1), halo, 1, -1)
+    copies[6 + GX_DOWN].wait_recv()
+    copies[6 + GX_UP].wait_recv()
+    halo = unpack(face_in[4 + GX_DOWN], face_in[4 + GX_UP], 0)
+    total = hops_across(total, pair_x, halo, 0, -1)
+    copies[6 + SA_DOWN].wait_recv()
+    copies[6 + SA_UP].wait_recv()
     second = 2.0 * cheb_scale * cheb_scale
+
+    def spread(ref):
+        for site in range(4):
+            for h in range(2):
+                block = pl.ds(h * 96 + site * 24, 24)
+                ref[pl.ds(site * 24, 24), pl.ds(128 * h, 128)] = natural[block, :]
+
     for a in range(4):
         scale = from_up if a < 2 else from_down
         for part in range(2):
@@ -307,20 +406,21 @@
                 - 0.5 * total[a][part]
                 - scale * chiral_in[24 + row : 24 + row + 3]
             )
-            value = value - 0.5 * field_v[row : row + 3]
+            value = value + cheb_shift * field_v[row : row + 3]
             for c in range(3):
-                mirror_out_row = pl.ds(row + c, 8, stride=24)
-                uin[mirror_out_row, :] = value[c]
-    copies[1, MIRROR].wait_recv()
-    rows = lax.broadcasted_iota(jnp.int32, (24, 128), 0)
-    five = jnp.where(rows < 12, cheb_scale, -cheb_scale).astype(jnp.float32)
-    for site in range(4):
-        for h in range(2):
-            block = pl.ds(h * 96 + site * 24, 24)
-            hv = five * mirror_in[block, :]
-            place = (pl.ds(site * 24, 24), pl.ds(128 * h, 128))
-            once_ref[place] = hv
-            twice_ref[place] = uin[block, :]
+                natural[pl.ds(row + c, 8, stride=24), :] = value[c]
+    spread(rest_ref)
+    for index in (MAIN, RELAY_UP, RELAY_DOWN):
+        copies[index].wait_recv()
+    total = halo_terms(unpack(relay_in[0], relay_in[1], 1))
+    for a in range(4):
+        scale = cheb_scale if a < 2 else -cheb_scale
+        for part in range(2):
+            row = a * 6 + part * 3
+            value = scale * (mirror_in[row : row + 3] - 0.5 * total[a][part])
+            for c in range(3):
+                natural[pl.ds(row + c, 8, stride=24), :] = value[c]
+    spread(mirrored_ref)
     for copy in copies.values():
         copy.wait_send()
 
@@ -340,14 +440,17 @@
             pltpu.VMEM((24, 8, 128), jnp.float32),
             pltpu.VMEM((72, 8, 128), jnp.float32),
             pltpu.VMEM((24, 8, 128), jnp.float32),
-            pltpu.VMEM((192, 128), jnp.float32),
-            pltpu.VMEM((192, 128), jnp.float32),
+            pltpu.VMEM((24, 8, 128), jnp.float32),
             pltpu.VMEM((8, 6, 8, 128), jnp.float32),
             pltpu.VMEM((8, 6, 8, 128), jnp.float32),
             pltpu.VMEM((48, 8, 128), jnp.float32),
+            pltpu.VMEM((24, 8, 128), jnp.float32),
+            pltpu.VMEM((2, 6, 8, 128), jnp.float32),
+            pltpu.VMEM((192, 128), jnp.float32),
             pltpu.SemaphoreType.DMA((4,)),
-            pltpu.SemaphoreType.DMA((14,)),
-            pltpu.SemaphoreType.DMA((14,)),
+            pltpu.SemaphoreType.REGULAR((7,)),
+            pltpu.SemaphoreType.DMA((15,)),
+            pltpu.SemaphoreType.DMA((15,)),
         ],
         compiler_params=pltpu.CompilerParams(collective_id=0, has_side_effects=True),
         name="chebyshev",

time: 35.7 us -> 33.9 us (0.950)
  the two profiles are of different devices: /device:TPU:1 before, /device:TPU:32 now
where the time goes in v3:
time: 33.9 us; the launch traced here: 33.8 us
  Pallas kernels  32.4 us (96%)
  other arithmetic  0.69 us (2%)
  between operations  0.65 us (2%)
    pallas_call x1, Pallas kernels, per_device(): pl.pallas_call(kernel, out_shape=(shape, shape), in_specs=[pl.BlockSpec(m...  32.4 us
    sub x1, other arithmetic, per_device(): twice = rest - 2.0 * hv  0.69 us

profile of v3, /device:TPU:32, one launch (start us, length us, event | category | flops | bytes accessed | tf_op | source)
XLA Modules:
  0.0 33.8 jit_solution(4263449362679590838)
XLA Ops:
  0.6 0.0 copy-start
  0.6 32.4 %chebyshev.1 = (f32[96,256]{1,0:T(8,128)S(1)}, f32[96,256]{1,0:T(8,128)S(1)}) custom-call(f32[96,256]{1,0:T(8,128)} %bitcast.5, f32[288,256]{1,0:T(8,128)} %bitcast.6), custom_call_target="tpu_custom_call" | custom-call | tf_op jit(solution)/shard_map/chebyshev/pallas_call | solution.py:432
  33.1 0.0 copy-done
  33.1 0.7 %multiply_subtract_fusion = (f32[96,256]{1,0:T(8,128)}, f32[96,256]{1,0:T(8,128)}) fusion(f32[96,256]{1,0:T(8,128)S(1)} %get-tuple-element.5, f32[96,256]{1,0:T(8,128)S(1)} %get-tuple-element.4, f32[1,2,2,24,256]{4,3,2,1,0:T(8,128)S(1)} %copy-done), kind=kLoop, calls=%fused_computation | loop fusion | flops 98304 | bytes 491520 | tf_op jit(solution)/shard_map/sub | solution.py:460
Async XLA Ops:
  0.6 32.4 %copy-start = (f32[1,2,2,24,256]{4,3,2,1,0:T(8,128)S(1)}, f32[1,2,2,24,256]{4,3,2,1,0:T(8,128)}, u32[]{:S(2)}) copy-start(f32[1,2,2,24,256]{4,3,2,1,0:T(8,128)} %param.2) | copy-start | bytes 294916

commit v4 on v3

--- a/solution.py
+++ b/solution.py
@@ -165,7 +165,11 @@
     )
 
     def rank(axis, index):
-        return index + 1 - 2 * lax.rem(index, 2) if axis == "gx" else index
+        if axis == "gx":
+            return index + 1 - 2 * lax.rem(index, 2)
+        if axis == "gy":
+            return jnp.where(index < 2, index, 5 - index)
+        return index
 
     first = []
     lowest = me["gy"] == 0

time: 33.9 us -> 31.4 us (0.926)
  the two profiles are of different devices: /device:TPU:32 before, /device:TPU:1 now
where the time goes in v4:
time: 31.4 us; the launch traced here: 30.8 us
  Pallas kernels  29.5 us (94%)
  other arithmetic  0.69 us (2%)
  between operations  0.65 us (2%)
    pallas_call x1, Pallas kernels, per_device(): pl.pallas_call(kernel, out_shape=(shape, shape), in_specs=[pl.BlockSpec(m...  29.5 us
    sub x1, other arithmetic, per_device(): twice = rest - 2.0 * hv  0.69 us

profile of v4, /device:TPU:1, one launch (start us, length us, event | category | flops | bytes accessed | tf_op | source)
XLA Modules:
  0.0 30.8 jit_solution(7402304793361831381)
XLA Ops:
  0.6 0.0 copy-start
  0.6 29.5 %chebyshev.1 = (f32[96,256]{1,0:T(8,128)S(1)}, f32[96,256]{1,0:T(8,128)S(1)}) custom-call(f32[96,256]{1,0:T(8,128)} %bitcast.5, f32[288,256]{1,0:T(8,128)} %bitcast.6), custom_call_target="tpu_custom_call" | custom-call | tf_op jit(solution)/shard_map/chebyshev/pallas_call | solution.py:436
  30.1 0.0 copy-done
  30.1 0.7 %multiply_subtract_fusion = (f32[96,256]{1,0:T(8,128)}, f32[96,256]{1,0:T(8,128)}) fusion(f32[96,256]{1,0:T(8,128)S(1)} %get-tuple-element.5, f32[96,256]{1,0:T(8,128)S(1)} %get-tuple-element.4, f32[1,2,2,24,256]{4,3,2,1,0:T(8,128)S(1)} %copy-done), kind=kLoop, calls=%fused_computation | loop fusion | flops 98304 | bytes 491520 | tf_op jit(solution)/shard_map/sub | solution.py:464
Async XLA Ops:
  0.6 29.5 %copy-start = (f32[1,2,2,24,256]{4,3,2,1,0:T(8,128)S(1)}, f32[1,2,2,24,256]{4,3,2,1,0:T(8,128)}, u32[]{:S(2)}) copy-start(f32[1,2,2,24,256]{4,3,2,1,0:T(8,128)} %param.2) | copy-start | bytes 294916

commit v5 on v4

--- a/solution.py
+++ b/solution.py
@@ -136,6 +136,7 @@
     links,
     field_p,
     field_g,
+    field_r,
     face_out,
     face_in,
     chiral_in,
@@ -282,31 +283,30 @@
         total = expand(total, link_times(link, ahead, False), direction, -sign)
         return expand(total, behind, direction, sign)
 
-    def halo_terms(halo):
+    def halo_terms(halo, sign):
         low = mask["low"][1]
         ahead = [jnp.where(low, 0.0, halo[0][k]) for k in range(2)]
         behind = [jnp.where(low, halo[1][k], 0.0) for k in range(2)]
-        total = expand(nothing, link_times(link_of(links, 1), ahead, False), 1, -1)
-        return expand(total, behind, 1, 1)
+        total = expand(nothing, link_times(link_of(links, 1), ahead, False), 1, -sign)
+        return expand(total, behind, 1, sign)
 
     last = size["sa"] - 1
     from_down = jnp.where(me["sa"] == 0, -wall_mass, 1.0).astype(jnp.float32)
     from_up = jnp.where(me["sa"] == last, -wall_mass, 1.0).astype(jnp.float32)
     no_halo = ((0.0, 0.0), (0.0, 0.0))
 
-    for load in loads:
+    for load in (loads[0], loads[2]):
         load.wait()
     for r in range(24):
         field_v[r] = vin[pl.ds(r, 8, stride=24), :]
-    for r in range(72):
+    for load in (loads[1], loads[3]):
+        load.wait()
+    for r in range(18, 36):
         links[r] = uin[pl.ds(r, 8, stride=72), :]
 
     field = reader(field_v)
     pair_y = halves(field, 1, 1)
     pack(pair_y, 1, 0)
-    pair_x = halves(field, 0, 1)
-    pack(pair_x, 0, 0)
-
     count = jnp.int32(0)
     for way in range(7):
         count = count + jnp.where(first[way], 0, 1)
@@ -325,9 +325,24 @@
                 known_sem.at[BACK[way]], inc=1, device_id=device, device_id_type=MESH
             )
 
-    for way in (GX_DOWN, GX_UP, SA_UP, SA_DOWN):
-        meet(way)
-        copies[way].start()
+    for r in (*range(18), *range(36, 72)):
+        links[r] = uin[pl.ds(r, 8, stride=72), :]
+    pair_x = halves(field, 0, 1)
+    pack(pair_x, 0, 0)
+    near = (GX_DOWN, GX_UP, SA_UP, SA_DOWN)
+    for way in near:
+
+        @pl.when(jnp.logical_not(first[way]))
+        def _(way=way):
+            copies[way].start()
+
+    for way in near:
+
+        @pl.when(first[way])
+        def _(way=way):
+            pl.semaphore_wait(known_sem.at[way], 1)
+            copies[way].start()
+
     total = hops_local(nothing, field, 1)
     total = hops_across(total, pair_y, no_halo, 1, 1)
     copies[GX_DOWN].wait_recv()
@@ -345,14 +360,20 @@
                 - 0.5 * total[a][part]
                 - scale * chiral_in[row : row + 3]
             )
-    meet(MIRROR)
-    copies[MAIN].start()
     pack(halves(reader(field_p), 1, -1), 1, 1)
     for way in (GY_UP, GY_DOWN):
 
         @pl.when(jnp.logical_not(first[way]))
         def _(way=way):
             copies[6 + way].start()
+
+    soon = me["gy"] == 0
+
+    meet(MIRROR)
+
+    @pl.when(soon)
+    def _():
+        copies[MAIN].start()
 
     for way, relay in ((GY_UP, RELAY_UP), (GY_DOWN, RELAY_DOWN)):
 
@@ -365,8 +386,12 @@
         copies[BACK[way]].wait_recv()
         copies[relay].start()
 
+    @pl.when(jnp.logical_not(soon))
+    def _():
+        copies[MAIN].start()
+
     halo = unpack(face_in[GY_DOWN], face_in[GY_UP], 1)
-    total = halo_terms(halo)
+    total = halo_terms(halo, 1)
     for a in range(4):
         for part in range(2):
             row = a * 6 + part * 3
@@ -379,14 +404,7 @@
     copies[6 + GX_DOWN].start()
     copies[6 + GX_UP].start()
     total = hops_local(nothing, field, -1)
-    copies[6 + GY_DOWN].wait_recv()
-    copies[6 + GY_UP].wait_recv()
-    halo = unpack(face_in[4 + GY_DOWN], face_in[4 + GY_UP], 1)
-    halo = (
-        [halo[0][k] - pair_y[1][k] for k in range(2)],
-        [halo[1][k] - pair_y[0][k] for k in range(2)],
-    )
-    total = hops_across(total, halves(field, 1, -1), halo, 1, -1)
+    total = hops_across(total, halves(field, 1, -1), no_halo, 1, -1)
     copies[6 + GX_DOWN].wait_recv()
     copies[6 + GX_UP].wait_recv()
     halo = unpack(face_in[4 + GX_DOWN], face_in[4 + GX_UP], 0)
@@ -410,13 +428,10 @@
                 - 0.5 * total[a][part]
                 - scale * chiral_in[24 + row : 24 + row + 3]
             )
-            value = value + cheb_shift * field_v[row : row + 3]
-            for c in range(3):
-                natural[pl.ds(row + c, 8, stride=24), :] = value[c]
-    spread(rest_ref)
+            field_r[row : row + 3] = value + cheb_shift * field_v[row : row + 3]
     for index in (MAIN, RELAY_UP, RELAY_DOWN):
         copies[index].wait_recv()
-    total = halo_terms(unpack(relay_in[0], relay_in[1], 1))
+    total = halo_terms(unpack(relay_in[0], relay_in[1], 1), 1)
     for a in range(4):
         scale = cheb_scale if a < 2 else -cheb_scale
         for part in range(2):
@@ -425,6 +440,21 @@
             for c in range(3):
                 natural[pl.ds(row + c, 8, stride=24), :] = value[c]
     spread(mirrored_ref)
+    copies[6 + GY_DOWN].wait_recv()
+    copies[6 + GY_UP].wait_recv()
+    halo = unpack(face_in[4 + GY_DOWN], face_in[4 + GY_UP], 1)
+    halo = (
+        [halo[0][k] - pair_y[1][k] for k in range(2)],
+        [halo[1][k] - pair_y[0][k] for k in range(2)],
+    )
+    late = halo_terms(halo, -1)
+    for a in range(4):
+        for part in range(2):
+            row = a * 6 + part * 3
+            value = field_r[row : row + 3] - 0.5 * second * late[a][part]
+            for c in range(3):
+                natural[pl.ds(row + c, 8, stride=24), :] = value[c]
+    spread(rest_ref)
     for copy in copies.values():
         copy.wait_send()
 
@@ -443,6 +473,7 @@
             pltpu.VMEM((576, 128), jnp.float32),
             pltpu.VMEM((24, 8, 128), jnp.float32),
             pltpu.VMEM((72, 8, 128), jnp.float32),
+            pltpu.VMEM((24, 8, 128), jnp.float32),
             pltpu.VMEM((24, 8, 128), jnp.float32),
             pltpu.VMEM((24, 8, 128), jnp.float32),
             pltpu.VMEM((8, 6, 8, 128), jnp.float32),

time: 31.4 us -> 31.2 us (level)
  the two profiles are of different devices: /device:TPU:1 before, /device:TPU:32 now
where the time goes in v5:
time: 31.2 us; the launch traced here: 31 us
  Pallas kernels  29.7 us (95%)
  other arithmetic  0.69 us (2%)
  between operations  0.65 us (2%)
    pallas_call x1, Pallas kernels, per_device(): pl.pallas_call(kernel, out_shape=(shape, shape), in_specs=[pl.BlockSpec(m...  29.7 us
    sub x1, other arithmetic, per_device(): twice = rest - 2.0 * hv  0.69 us

profile of v5, /device:TPU:32, one launch (start us, length us, event | category | flops | bytes accessed | tf_op | source)
XLA Modules:
  0.0 31.0 jit_solution(7639473357959750541)
XLA Ops:
  0.6 0.0 copy-start
  0.6 29.7 %chebyshev.1 = (f32[96,256]{1,0:T(8,128)S(1)}, f32[96,256]{1,0:T(8,128)S(1)}) custom-call(f32[96,256]{1,0:T(8,128)} %bitcast.5, f32[288,256]{1,0:T(8,128)} %bitcast.6), custom_call_target="tpu_custom_call" | custom-call | tf_op jit(solution)/shard_map/chebyshev/pallas_call | solution.py:466
  30.3 0.0 copy-done
  30.3 0.7 %multiply_subtract_fusion = (f32[96,256]{1,0:T(8,128)}, f32[96,256]{1,0:T(8,128)}) fusion(f32[96,256]{1,0:T(8,128)S(1)} %get-tuple-element.5, f32[96,256]{1,0:T(8,128)S(1)} %get-tuple-element.4, f32[1,2,2,24,256]{4,3,2,1,0:T(8,128)S(1)} %copy-done), kind=kLoop, calls=%fused_computation | loop fusion | flops 98304 | bytes 491520 | tf_op jit(solution)/shard_map/sub | solution.py:495
Async XLA Ops:
  0.6 29.7 %copy-start = (f32[1,2,2,24,256]{4,3,2,1,0:T(8,128)S(1)}, f32[1,2,2,24,256]{4,3,2,1,0:T(8,128)}, u32[]{:S(2)}) copy-start(f32[1,2,2,24,256]{4,3,2,1,0:T(8,128)} %param.2) | copy-start | bytes 294916

commit v6 on v5

--- a/solution.py
+++ b/solution.py
@@ -166,8 +166,6 @@
     )
 
     def rank(axis, index):
-        if axis == "gx":
-            return index + 1 - 2 * lax.rem(index, 2)
         if axis == "gy":
             return jnp.where(index < 2, index, 5 - index)
         return index
@@ -307,6 +305,10 @@
     field = reader(field_v)
     pair_y = halves(field, 1, 1)
     pack(pair_y, 1, 0)
+    for r in (*range(18), *range(36, 72)):
+        links[r] = uin[pl.ds(r, 8, stride=72), :]
+    pair_x = halves(field, 0, 1)
+    pack(pair_x, 0, 0)
     count = jnp.int32(0)
     for way in range(7):
         count = count + jnp.where(first[way], 0, 1)
@@ -325,10 +327,6 @@
                 known_sem.at[BACK[way]], inc=1, device_id=device, device_id_type=MESH
             )
 
-    for r in (*range(18), *range(36, 72)):
-        links[r] = uin[pl.ds(r, 8, stride=72), :]
-    pair_x = halves(field, 0, 1)
-    pack(pair_x, 0, 0)
     near = (GX_DOWN, GX_UP, SA_UP, SA_DOWN)
     for way in near:
 

time: 31.2 us -> 31.2 us (level)
  no operation moved by 1% of the time
where the time goes in v6:
time: 31.2 us; the launch traced here: 31 us
  Pallas kernels  29.7 us (95%)
  other arithmetic  0.69 us (2%)
  between operations  0.65 us (2%)
    pallas_call x1, Pallas kernels, per_device(): pl.pallas_call(kernel, out_shape=(shape, shape), in_specs=[pl.BlockSpec(m...  29.7 us
    sub x1, other arithmetic, per_device(): twice = rest - 2.0 * hv  0.69 us

profile of v6, /device:TPU:32, one launch (start us, length us, event | category | flops | bytes accessed | tf_op | source)
XLA Modules:
  0.0 31.0 jit_solution(1911985660590800316)
XLA Ops:
  0.6 0.0 copy-start
  0.6 29.7 %chebyshev.1 = (f32[96,256]{1,0:T(8,128)S(1)}, f32[96,256]{1,0:T(8,128)S(1)}) custom-call(f32[96,256]{1,0:T(8,128)} %bitcast.5, f32[288,256]{1,0:T(8,128)} %bitcast.6), custom_call_target="tpu_custom_call" | custom-call | tf_op jit(solution)/shard_map/chebyshev/pallas_call | solution.py:464
  30.3 0.0 copy-done
  30.3 0.7 %multiply_subtract_fusion = (f32[96,256]{1,0:T(8,128)}, f32[96,256]{1,0:T(8,128)}) fusion(f32[96,256]{1,0:T(8,128)S(1)} %get-tuple-element.5, f32[96,256]{1,0:T(8,128)S(1)} %get-tuple-element.4, f32[1,2,2,24,256]{4,3,2,1,0:T(8,128)S(1)} %copy-done), kind=kLoop, calls=%fused_computation | loop fusion | flops 98304 | bytes 491520 | tf_op jit(solution)/shard_map/sub | solution.py:493
Async XLA Ops:
  0.6 29.7 %copy-start = (f32[1,2,2,24,256]{4,3,2,1,0:T(8,128)S(1)}, f32[1,2,2,24,256]{4,3,2,1,0:T(8,128)}, u32[]{:S(2)}) copy-start(f32[1,2,2,24,256]{4,3,2,1,0:T(8,128)} %param.2) | copy-start | bytes 294916
